TPU v7x, 256 devices: a whole 4x4x8 slice. The times are simulated.
256 devices in a mesh: cube: 4 (over y), grid: 64 (over z, x, core).
Axes of the slice: x: 4, y: 4, z: 8, core: 2. Of those that a mesh axis runs over, the one named last changes fastest.
Arguments:
- root_inverse: float32 [4096, 4096], P('grid', 'cube'), may hold values from -0.09375 to 0.09375
- level_inverse: float32 [1024, 2048], P('grid', 'cube'), may hold values from -0.1875 to 0.1875
- coupling: float32 [4096, 2048], P('grid', 'cube'), may hold values from -0.1875 to 0.1875
- pattern: int32 [2, 32], replicated, may hold values 0 or 1
Outputs:
- root_cov: float32 [4096, 4096], P('grid', 'cube')
- cross_cov: float32 [4096, 2048], P('grid', 'cube')
- node_cov: float32 [1024, 2048], P('grid', 'cube')
All inputs are finite; a program needn't handle non-finite values.
Results may differ from a plain program's by a relative error of at most 0.0001.
Values sent between devices are 32-bit elements; how exact they have to be, the bound alone decides.
No kernel may reach another device: no remote copies, remote signals or barrier semaphores. Data moves between devices by JAX's collectives and lax.ppermute only.
A program may use at most 128 MiB of HBM per device.

v0:
```python
import jax
import jax.numpy as jnp
from jax import lax
from jax.sharding import PartitionSpec as P

BLK = 128
HIGHEST = lax.Precision.HIGHEST


def from_partner(value, axis, apart):
    return lax.ppermute(value, axis, [(i, i ^ 1 << apart) for i in range(lax.axis_size(axis))])


def product(left, right):
    return jnp.dot(left, right, precision=HIGHEST, preferred_element_type=jnp.float32)


def lower_piece(weights, row_start, col_start):
    rows = row_start + lax.broadcasted_iota(jnp.int32, weights.shape, 0)
    cols = col_start + lax.broadcasted_iota(jnp.int32, weights.shape, 1)
    below = jnp.where(cols < rows, weights, jnp.zeros_like(weights))
    return below + jnp.where(cols == rows, 1.0, 0.0).astype(jnp.float32)


def join_halves(own, other, half):
    first = jnp.concatenate([own, other], axis=1)
    second = jnp.concatenate([other, own], axis=1)
    return jnp.where(half == 0, first, second)


def on_device(root_inverse, level_inverse, coupling, pattern):
    grid_index = lax.axis_index("grid")
    cube_index = lax.axis_index("cube")
    node = cube_index // 2
    half = cube_index % 2
    root_rows_dev, root_cols_dev = root_inverse.shape
    node_rows_dev, half_width = level_inverse.shape
    root_lower = lower_piece(root_inverse, grid_index * root_rows_dev, cube_index * root_cols_dev)
    node_lower = lower_piece(level_inverse, grid_index * node_rows_dev, half * half_width)
    row_ids = grid_index * root_rows_dev + jnp.arange(root_rows_dev, dtype=jnp.int32)
    block_count = pattern.shape[1]
    chosen = jnp.where(node == 0, pattern[0], pattern[1]).astype(jnp.float32)
    onehot = (
        jnp.arange(block_count, dtype=jnp.int32)[None, :] == (row_ids // BLK)[:, None]
    ).astype(jnp.float32)
    row_mask = jnp.sum(onehot * chosen[None, :], axis=1)[:, None]
    masked_coupling = coupling * row_mask
    lower_rows = lax.all_gather(root_lower, "cube", axis=1, tiled=True)
    root_cov = lax.psum_scatter(
        product(lower_rows.T, root_lower), "grid", scatter_dimension=0, tiled=True
    )
    cov_rows = lax.all_gather(root_cov, "cube", axis=1, tiled=True)
    other_coupling, other_lower = from_partner((masked_coupling, node_lower), "cube", 0)
    coupling_full = join_halves(masked_coupling, other_coupling, half)
    lower_full = join_halves(node_lower, other_lower, half)
    factor = product(coupling_full, lax.all_gather(node_lower, "grid", axis=0, tiled=True))
    cross = lax.psum_scatter(-product(cov_rows.T, factor), "grid", scatter_dimension=0, tiled=True)
    cross = cross * row_mask
    other_cross = from_partner(cross, "cube", 0)
    left_rows = join_halves(cross, other_cross, half)
    first = product(lower_full.T, node_lower)
    node_cov = lax.psum_scatter(
        first - product(left_rows.T, factor), "grid", scatter_dimension=0, tiled=True
    )
    return (root_cov, cross, node_cov)


def solution(mesh):
    placed = (P("grid", "cube"), P("grid", "cube"), P("grid", "cube"), P())
    return jax.shard_map(
        on_device,
        mesh=mesh,
        in_specs=placed,
        out_specs=(P("grid", "cube"), P("grid", "cube"), P("grid", "cube")),
        check_vma=False,
    )
```

profile of v0, /device:TPU:8, one launch (start us, length us, event | category | flops | bytes accessed | tf_op | source)
XLA Modules:
  0.0 671.0 jit_solution(15860373816275779728)
XLA Ops:
  7.2 0.0 all-gather.4.cloned.1.call-start
  7.2 1.8 select_add_fusion
  9.0 0.0 all-gather.4.cloned.1.call-update
  9.0 0.0 reduce-scatter.4.cloned.1.call-start
  9.1 29.8 %all-gather.4.cloned.1.call-done = f32[64,4096]{1,0:T(8,128)} async-done(((f32[64,1024]{1,0:T(8,128)}), f32[64,4096]{1,0:T(8,128)}) %all-gather.4.cloned.1.call-update) | async-done | bytes 1048592 | tf_op jit(solution)/shard_map/all_gather | solution.py:48
  38.9 16.9 %fusion.25 = f32[4096,1024]{1,0:T(8,128)} fusion(f32[64,4096]{1,0:T(8,128)} %all-gather.4.cloned.1.call-done, f32[64,1024]{1,0:T(8,128)} %select_add_fusion), kind=kOutput, calls=%fused_computation.45 | convolution fusion | flops 3221225472 | bytes 18087936 | tf_op jit(solution)/shard_map/dot_general | solution.py:15
  55.8 0.0 copy-start.3
  55.8 0.0 copy-start.4
  55.8 0.0 copy-start.2
  55.8 0.0 reduce-scatter.4.cloned.1.call-update
  55.8 0.0 all-gather.8.cloned.1.call-start
  55.9 0.6 copy-done.3
  56.6 0.7 select_add_fusion.1
  57.2 0.0 all-gather.8.cloned.1.call-update
  57.3 0.0 all-gather.6.cloned.1.call-start
  57.3 189.2 %reduce-scatter.4.cloned.1.call-done = f32[64,1024]{1,0:T(8,128)} async-done(((f32[4096,1024]{1,0:T(8,128)}), f32[64,1024]{1,0:T(8,128)}) %reduce-scatter.4.cloned.1.call-update) | async-done | bytes 262160 | tf_op jit(solution)/shard_map/reduce_scatter | solution.py:49
  246.6 0.0 all-gather.6.cloned.1.call-update
  246.6 0.0 reduce-scatter.6.cloned.1.call-start
  246.7 0.0 copy-done.4
  246.7 0.1 select_reduce_fusion
  246.8 0.0 copy-done.2
  246.8 0.1 broadcast_multiply_fusion.1
  246.9 0.6 collective-permute-start
  247.4 4.5 collective-permute-done
  251.9 73.5 %all-gather.8.cloned.1.call-done = f32[1024,512]{1,0:T(8,128)} async-done(((f32[16,512]{1,0:T(8,128)}), f32[1024,512]{1,0:T(8,128)}) %all-gather.8.cloned.1.call-update) | async-done | bytes 2097168 | tf_op jit(solution)/shard_map/all_gather | solution.py:56
  325.5 3.0 fusion
  328.4 22.7 %all-gather.6.cloned.1.call-done = f32[64,4096]{1,0:T(8,128)} async-done(((f32[64,1024]{1,0:T(8,128)}), f32[64,4096]{1,0:T(8,128)}) %all-gather.6.cloned.1.call-update) | async-done | bytes 1048592 | tf_op jit(solution)/shard_map/all_gather | solution.py:52
  351.1 10.0 %convolution_negate_fusion = f32[4096,512]{1,0:T(8,128)} fusion(f32[64,4096]{1,0:T(8,128)} %all-gather.6.cloned.1.call-done, f32[64,512]{1,0:T(8,128)S(1)} %fusion), kind=kOutput, calls=%fused_computation | convolution fusion | flops 1612709888 | bytes 9568256 | tf_op jit(solution)/shard_map/dot_general | solution.py:15
  361.1 0.0 copy-start.1
  361.1 0.0 reduce-scatter.6.cloned.1.call-update
  361.1 0.0 reduce-scatter.8.cloned.1.call-start
  361.2 152.8 %reduce-scatter.6.cloned.1.call-done = f32[64,512]{1,0:T(8,128)} async-done(((f32[4096,512]{1,0:T(8,128)}), f32[64,512]{1,0:T(8,128)}) %reduce-scatter.6.cloned.1.call-update) | async-done | bytes 131088 | tf_op jit(solution)/shard_map/reduce_scatter | solution.py:57
  514.0 1.0 broadcast_multiply_fusion
  514.9 0.0 copy-start
  514.9 0.6 collective-permute-start.2
  515.6 0.0 copy-done.1
  515.6 1.5 collective-permute-start.1
  517.1 2.9 collective-permute-done.2
  520.0 1.8 fusion.6
  521.9 0.0 collective-permute-done.1
  521.9 3.2 convolution_subtract_fusion
  525.1 0.0 copy-done
  525.1 0.0 reduce-scatter.8.cloned.1.call-update
  525.1 139.1 %reduce-scatter.8.cloned.1.call-done = f32[16,512]{1,0:T(8,128)} async-done(((f32[1024,512]{1,0:T(8,128)}), f32[16,512]{1,0:T(8,128)}) %reduce-scatter.8.cloned.1.call-update) | async-done | bytes 32784 | tf_op jit(solution)/shard_map/reduce_scatter | solution.py:62
  (6 shorter events, 0.0 us)
Async XLA Ops:
  7.2 31.7 %all-gather.4.cloned.1.call-start = ((), (), s32[]{:S(2)}) async-start(), calls=%async_computation.3 | async-start | bytes 1310720 | tf_op jit(solution)/shard_map/all_gather | solution.py:48
  9.0 237.5 %reduce-scatter.4.cloned.1.call-start = ((), (), s32[]{:S(2)}) async-start(), calls=%async_computation.4 | async-start | bytes 17039360 | tf_op jit(solution)/shard_map/reduce_scatter | solution.py:49
  55.8 0.8 copy-start.3
  55.8 190.9 %copy-start.4 = (s32[2,32]{1,0:T(2,128)S(1)}, s32[2,32]{1,0:T(2,128)}, u32[]{:S(2)}) copy-start(s32[2,32]{1,0:T(2,128)} %param.7) | copy-start | bytes 772
  55.8 191.0 %copy-start.2 = (f32[64,512]{1,0:T(8,128)S(1)}, f32[64,512]{1,0:T(8,128)}, u32[]{:S(2)}) copy-start(f32[64,512]{1,0:T(8,128)} %param.6) | copy-start | bytes 393220
  55.8 269.6 %all-gather.8.cloned.1.call-start = ((), (), s32[]{:S(2)}) async-start(), calls=%async_computation.6 | async-start | bytes 2129920 | tf_op jit(solution)/shard_map/all_gather | solution.py:56
  57.3 293.8 %all-gather.6.cloned.1.call-start = ((), (), s32[]{:S(2)}) async-start(), calls=%async_computation.5 | async-start | bytes 1310720 | tf_op jit(solution)/shard_map/all_gather | solution.py:52
  246.6 267.4 %reduce-scatter.6.cloned.1.call-start = ((), (), s32[]{:S(2)}) async-start(), calls=%async_computation.7 | async-start | bytes 8519680 | tf_op jit(solution)/shard_map/reduce_scatter | solution.py:57
  246.9 5.1 collective-permute-start
  361.1 154.5 %copy-start.1 = (f32[16,512]{1,0:T(8,128)S(1)}, f32[16,512]{1,0:T(8,128)}, u32[]{:S(2)}) copy-start(f32[16,512]{1,0:T(8,128)} %select_add_fusion.1) | copy-start | bytes 98308
  361.1 303.0 %reduce-scatter.8.cloned.1.call-start = ((), (), s32[]{:S(2)}) async-start(), calls=%async_computation.8 | async-start | bytes 2129920 | tf_op jit(solution)/shard_map/reduce_scatter | solution.py:62
  514.9 10.1 %copy-start = (f32[64,512]{1,0:T(8,128)}, f32[64,512]{1,0:T(8,128)S(1)}, u32[]{:S(2)}) copy-start(f32[64,512]{1,0:T(8,128)S(1)} %broadcast_multiply_fusion) | copy-start | bytes 393220
  514.9 5.1 collective-permute-start.2
  515.6 6.3 collective-permute-start.1
Sparse Core Ops, SparseCore 0:
  10.4 28.4 all-gather.3
  56.0 190.5 reduce-scatter.3
  249.9 75.4 all-gather.7
  327.7 23.3 all-gather.5
  361.3 152.6 reduce-scatter.5
  525.2 138.8 reduce-scatter.7
where the time goes:
time: 671 us
  waiting for transfers between devices  615 us (92%)
  matrix products  34.9 us (5%)
  between operations  14.2 us (2%)
    reduce_scatter x1, waiting for transfers between devices, on_device(): lax.psum_scatter(product(lower_rows.T, root_lower), 'grid', scatter_dimen...  189 us
    reduce_scatter x1, waiting for transfers between devices, on_device(): lax.psum_scatter(-product(cov_rows.T, factor), 'grid', scatter_dimension=...  153 us
    reduce_scatter x1, waiting for transfers between devices, on_device(): lax.psum_scatter(first - product(left_rows.T, factor), 'grid', scatter_di...  139 us
    all_gather x1, waiting for transfers between devices, on_device(): lax.all_gather(node_lower, 'grid', axis=0, tiled=True)  73.5 us
    dot_general x5, matrix products, product(): jnp.dot(left, right, precision=HIGHEST, preferred_element_type=jnp.float32)  34.9 us
    all_gather x1, waiting for transfers between devices, on_device(): lower_rows = lax.all_gather(root_lower, 'cube', axis=1, tiled=True)  29.8 us
    all_gather x1, waiting for transfers between devices, on_device(): cov_rows = lax.all_gather(root_cov, 'cube', axis=1, tiled=True)  22.7 us
  transfers between devices with their start and end apart: 9, of which 8 were waited for; matrix products, arithmetic and copies ran while one was open for 1% of the time, Pallas kernels for 0%

commit v1 on v0

--- a/solution.py
+++ b/solution.py
@@ -2,9 +2,36 @@
 import jax.numpy as jnp
 from jax import lax
 from jax.sharding import PartitionSpec as P
+from jax.lax import axis_index, axis_size, ppermute
 
 BLK = 128
 HIGHEST = lax.Precision.HIGHEST
+
+
+def meet_masks_by_axis(content, dim_k):
+    d_next = list(content.shape[1:])
+    d_next[dim_k] *= content.shape[0]
+    return jnp.moveaxis(content, 0, dim_k).reshape(d_next)
+
+
+def remake_the_windows(field, mesh_name, array_axis):
+    cores_n = axis_size(mesh_name)
+    frames = [(dev, (dev + 1) % cores_n) for dev in range(cores_n)]
+    pieces_in = [(dev_i, j) for j, dev_i in frames]
+    wide_out, aux = ([], [])
+    for jj in range(cores_n - 1):
+        if jj % 2 == 0:
+            piece_out = ppermute(wide_out[-1] if wide_out else field, mesh_name, perm=frames)
+            wide_out.append(piece_out)
+        else:
+            x_next = ppermute(aux[-1] if aux else field, mesh_name, perm=pieces_in)
+            aux.append(x_next)
+    val2 = jnp.stack([*wide_out[::-1], field, *aux], axis=0)
+    mixed_arr = axis_index(mesh_name)
+    val = len(wide_out)
+    known = mixed_arr - val
+    val2 = val2[(jnp.arange(cores_n) - known) % cores_n]
+    return meet_masks_by_axis(val2, array_axis)
 
 
 def from_partner(value, axis, apart):
@@ -49,7 +76,7 @@
     root_cov = lax.psum_scatter(
         product(lower_rows.T, root_lower), "grid", scatter_dimension=0, tiled=True
     )
-    cov_rows = lax.all_gather(root_cov, "cube", axis=1, tiled=True)
+    cov_rows = remake_the_windows(root_cov, "cube", 1)
     other_coupling, other_lower = from_partner((masked_coupling, node_lower), "cube", 0)
     coupling_full = join_halves(masked_coupling, other_coupling, half)
     lower_full = join_halves(node_lower, other_lower, half)

time: 671 us -> 644 us (0.960)
  waiting for transfers between devices: 615 us -> 584 us
    all_gather x1 -> x0, waiting for transfers between devices: 22.7 us -> none  [on_device(): cov_rows = lax.all_gather(root_cov, 'cube', axis=1, tiled=True)]
  transfers between devices with their start and end apart: 9 -> 11, of which waited for: 8 -> 7; matrix products, arithmetic and copies ran while one was open for 1% -> 1% of each run, Pallas kernels for 0% -> 0%
where the time goes in v1:
time: 644 us
  waiting for transfers between devices  584 us (91%)
  matrix products  33.9 us (5%)
  between operations  14 us (2%)
  starting transfers between devices  7.42 us (1%)
    reduce_scatter x1, waiting for transfers between devices, on_device(): lax.psum_scatter(product(lower_rows.T, root_lower), 'grid', scatter_dimen...  189 us
    reduce_scatter x1, waiting for transfers between devices, on_device(): lax.psum_scatter(-product(cov_rows.T, factor), 'grid', scatter_dimension=...  149 us
    reduce_scatter x1, waiting for transfers between devices, on_device(): lax.psum_scatter(first - product(left_rows.T, factor), 'grid', scatter_di...  139 us
    all_gather x1, waiting for transfers between devices, on_device(): lax.all_gather(node_lower, 'grid', axis=0, tiled=True)  68.1 us
    dot_general x5, matrix products, product(): jnp.dot(left, right, precision=HIGHEST, preferred_element_type=jnp.float32)  33.9 us
    all_gather x1, waiting for transfers between devices, on_device(): lower_rows = lax.all_gather(root_lower, 'cube', axis=1, tiled=True)  29.8 us
  transfers between devices with their start and end apart: 11, of which 7 were waited for; matrix products, arithmetic and copies ran while one was open for 1% of the time, Pallas kernels for 0%

profile of v1, /device:TPU:8, one launch (start us, length us, event | category | flops | bytes accessed | tf_op | source)
XLA Modules:
  0.0 644.2 jit_solution(3449174010722368417)
XLA Ops:
  7.2 0.0 all-gather.3.cloned.1.call-start
  7.2 1.8 select_add_fusion
  9.0 0.0 all-gather.3.cloned.1.call-update
  9.0 0.0 reduce-scatter.4.cloned.1.call-start
  9.1 29.8 %all-gather.3.cloned.1.call-done = f32[64,4096]{1,0:T(8,128)} async-done(((f32[64,1024]{1,0:T(8,128)}), f32[64,4096]{1,0:T(8,128)}) %all-gather.3.cloned.1.call-update) | async-done | bytes 1048592 | tf_op jit(solution)/shard_map/all_gather | solution.py:75
  38.9 16.9 %fusion.27 = f32[4096,1024]{1,0:T(8,128)} fusion(f32[64,4096]{1,0:T(8,128)} %all-gather.3.cloned.1.call-done, f32[64,1024]{1,0:T(8,128)} %select_add_fusion), kind=kOutput, calls=%fused_computation.54 | convolution fusion | flops 3221225472 | bytes 18087936 | tf_op jit(solution)/shard_map/dot_general | solution.py:42
  55.8 0.0 copy-start.4
  55.8 0.0 copy-start.5
  55.8 0.0 copy-start.3
  55.8 0.0 reduce-scatter.4.cloned.1.call-update
  55.8 0.0 all-gather.5.cloned.1.call-start
  55.9 0.6 copy-done.4
  56.6 0.7 select_add_fusion.1
  57.2 0.0 all-gather.5.cloned.1.call-update
  57.3 0.0 reduce-scatter.6.cloned.1.call-start
  57.4 0.0 copy-done.5
  57.4 0.1 select_reduce_fusion
  57.5 189.1 %reduce-scatter.4.cloned.1.call-done = f32[64,1024]{1,0:T(8,128)} async-done(((f32[4096,1024]{1,0:T(8,128)}), f32[64,1024]{1,0:T(8,128)}) %reduce-scatter.4.cloned.1.call-update) | async-done | bytes 262160 | tf_op jit(solution)/shard_map/reduce_scatter | solution.py:76
  246.6 0.0 copy-start.2
  246.6 1.4 collective-permute-start
  248.0 0.0 copy-done.3
  248.0 0.1 broadcast_multiply_fusion.1
  248.1 0.7 collective-permute-start.3
  248.8 1.5 collective-permute-start.2
  250.3 5.5 collective-permute-done
  255.8 1.5 collective-permute-start.1
  257.3 0.0 collective-permute-done.3
  257.3 68.1 %all-gather.5.cloned.1.call-done = f32[1024,512]{1,0:T(8,128)} async-done(((f32[16,512]{1,0:T(8,128)}), f32[1024,512]{1,0:T(8,128)}) %all-gather.5.cloned.1.call-update) | async-done | bytes 2097168 | tf_op jit(solution)/shard_map/all_gather | solution.py:83
  325.4 3.0 fusion
  328.4 0.0 collective-permute-done.2
  328.4 0.0 collective-permute-done.1
  328.4 0.0 copy-done.2
  328.5 0.1 pad_maximum_fusion
  328.6 0.6 gather_fusion
  329.2 0.1 copy.9
  329.3 9.0 %convolution_negate_fusion = f32[4096,512]{1,0:T(8,128)} fusion(f32[64,4096]{1,0:T(8,128)S(1)} %bitcast.18, f32[64,512]{1,0:T(8,128)S(1)} %fusion), kind=kOutput, calls=%fused_computation.1 | convolution fusion | flops 1612709888 | bytes 9568256 | tf_op jit(solution)/shard_map/dot_general | solution.py:42
  338.3 0.0 copy-start.1
  338.3 0.0 reduce-scatter.6.cloned.1.call-update
  338.3 0.0 reduce-scatter.8.cloned.1.call-start
  338.4 149.2 %reduce-scatter.6.cloned.1.call-done = f32[64,512]{1,0:T(8,128)} async-done(((f32[4096,512]{1,0:T(8,128)}), f32[64,512]{1,0:T(8,128)}) %reduce-scatter.6.cloned.1.call-update) | async-done | bytes 131088 | tf_op jit(solution)/shard_map/reduce_scatter | solution.py:84
  487.6 1.0 broadcast_multiply_fusion
  488.6 0.0 copy-start
  488.6 0.6 collective-permute-start.5
  489.2 0.0 copy-done.1
  489.2 1.5 collective-permute-start.4
  490.7 2.9 collective-permute-done.5
  493.7 1.8 fusion.6
  495.5 0.0 collective-permute-done.4
  495.5 3.2 convolution_subtract_fusion
  498.7 0.0 copy-done
  498.7 0.0 reduce-scatter.8.cloned.1.call-update
  498.7 139.0 %reduce-scatter.8.cloned.1.call-done = f32[16,512]{1,0:T(8,128)} async-done(((f32[1024,512]{1,0:T(8,128)}), f32[16,512]{1,0:T(8,128)}) %reduce-scatter.8.cloned.1.call-update) | async-done | bytes 32784 | tf_op jit(solution)/shard_map/reduce_scatter | solution.py:89
  (8 shorter events, 0.1 us)
Async XLA Ops:
  7.2 31.7 %all-gather.3.cloned.1.call-start = ((), (), s32[]{:S(2)}) async-start(), calls=%async_computation.3 | async-start | bytes 1310720 | tf_op jit(solution)/shard_map/all_gather | solution.py:75
  9.0 237.5 %reduce-scatter.4.cloned.1.call-start = ((), (), s32[]{:S(2)}) async-start(), calls=%async_computation.4 | async-start | bytes 17039360 | tf_op jit(solution)/shard_map/reduce_scatter | solution.py:76
  55.8 0.8 copy-start.4
  55.8 1.6 copy-start.5
  55.8 192.2 %copy-start.3 = (f32[64,512]{1,0:T(8,128)S(1)}, f32[64,512]{1,0:T(8,128)}, u32[]{:S(2)}) copy-start(f32[64,512]{1,0:T(8,128)} %param.6) | copy-start | bytes 393220
  55.8 269.6 %all-gather.5.cloned.1.call-start = ((), (), s32[]{:S(2)}) async-start(), calls=%async_computation.5 | async-start | bytes 2129920 | tf_op jit(solution)/shard_map/all_gather | solution.py:83
  57.3 430.3 %reduce-scatter.6.cloned.1.call-start = ((), (), s32[]{:S(2)}) async-start(), calls=%async_computation.6 | async-start | bytes 8519680 | tf_op jit(solution)/shard_map/reduce_scatter | solution.py:84
  246.6 81.9 %copy-start.2 = (f32[64,1024]{1,0:T(8,128)S(1)}, f32[64,1024]{1,0:T(8,128)}, u32[]{:S(2)}) copy-start(f32[64,1024]{1,0:T(8,128)} %reduce-scatter.4.cloned.1.call-done) | copy-start | bytes 786436
  246.6 9.3 %collective-permute-start = (f32[64,1024]{1,0:T(8,128)}, f32[64,1024]{1,0:T(8,128)S(1)}, u32[]{:S(2)}, u32[]{:S(2)}) collective-permute-start(f32[64,1024]{1,0:T(8,128)} %reduce-scatter.4.cloned.1.call-done), channel_id=1, source_target_pairs={{0,64},{64,128},{128,192},{192,0},{1,65},{65,129},{129,193},{193,1... | collective-permute-start | bytes 786440 | tf_op jit(solution)/shard_map/ppermute | solution.py:24
  248.1 9.3 %collective-permute-start.3 = (f32[64,512]{1,0:T(8,128)S(1)}, f32[64,512]{1,0:T(8,128)S(1)}, u32[]{:S(2)}, u32[]{:S(2)}) collective-permute-start(f32[64,512]{1,0:T(8,128)S(1)} %broadcast_multiply_fusion.1), channel_id=1, source_target_pairs={{0,64},{64,0},{128,192},{192,128},{1,65},{65,1},{129,193},{193,129... | collective-permute-start | bytes 393224 | tf_op jit(solution)/shard_map/ppermute | solution.py:38
  248.8 79.6 %collective-permute-start.2 = (f32[64,1024]{1,0:T(8,128)}, f32[64,1024]{1,0:T(8,128)S(1)}, u32[]{:S(2)}, u32[]{:S(2)}) collective-permute-start(f32[64,1024]{1,0:T(8,128)} %reduce-scatter.4.cloned.1.call-done), channel_id=1, source_target_pairs={{64,0},{128,64},{192,128},{0,192},{65,1},{129,65},{193,129},{1,193... | collective-permute-start | bytes 786440 | tf_op jit(solution)/shard_map/ppermute | solution.py:27
  255.8 72.6 %collective-permute-start.1 = (f32[64,1024]{1,0:T(8,128)S(1)}, f32[64,1024]{1,0:T(8,128)S(1)}, u32[]{:S(2)}, u32[]{:S(2)}) collective-permute-start(f32[64,1024]{1,0:T(8,128)S(1)} %collective-permute-done), channel_id=1, source_target_pairs={{0,64},{64,128},{128,192},{192,0},{1,65},{65,129},{129,193},{193,1... | collective-permute-start | bytes 786440 | tf_op jit(solution)/shard_map/ppermute | solution.py:24
  338.3 150.9 %copy-start.1 = (f32[16,512]{1,0:T(8,128)S(1)}, f32[16,512]{1,0:T(8,128)}, u32[]{:S(2)}) copy-start(f32[16,512]{1,0:T(8,128)} %select_add_fusion.1) | copy-start | bytes 98308
  338.3 299.4 %reduce-scatter.8.cloned.1.call-start = ((), (), s32[]{:S(2)}) async-start(), calls=%async_computation.7 | async-start | bytes 2129920 | tf_op jit(solution)/shard_map/reduce_scatter | solution.py:89
  488.6 10.1 %copy-start = (f32[64,512]{1,0:T(8,128)}, f32[64,512]{1,0:T(8,128)S(1)}, u32[]{:S(2)}) copy-start(f32[64,512]{1,0:T(8,128)S(1)} %broadcast_multiply_fusion) | copy-start | bytes 393220
  488.6 5.1 collective-permute-start.5
  489.2 6.3 collective-permute-start.4
Sparse Core Ops, SparseCore 0:
  10.4 28.4 all-gather.2
  56.0 190.5 reduce-scatter.3
  249.9 75.4 all-gather.4
  338.5 149.0 reduce-scatter.5
  498.8 138.8 reduce-scatter.7
